TPU v7x, 256 devices: a whole 4x4x8 slice. The times are simulated.
256 devices in a mesh: ctx: 64 (over z, x, y_hi), ch: 4 (over y_lo, core).
Axes of the slice: x: 4, y: 4 (y_hi: 2, y_lo: 2; y = y_hi * 2 + y_lo), z: 8, core: 2. Of those that a mesh axis runs over, the one named last changes fastest.
Arguments:
- query: bfloat16 [8192, 8192], P('ctx', 'ch'), may hold values from -6 to 6
- key: bfloat16 [8192, 8192], P('ctx', 'ch'), may hold values from -6 to 6
- value: bfloat16 [8192, 8192], P('ctx', 'ch'), may hold values from -6 to 6
- filter_taps: bfloat16 [1024, 512], P('ctx', 'ch'), may hold values from -0.1875 to 0.1875
- skip: float32 [8192], P('ch'), may hold values from -1 to 1
Outputs:
- gated: bfloat16 [8192, 8192], P('ctx', 'ch')
All inputs are finite; a program needn't handle non-finite values.
Results may differ from a plain program's by a relative error of at most 0.0085.
Values may be sent and summed in bfloat16 or wider, within the bound.
A program may use at most 192 MiB of HBM per device.

v0:
```python
import jax
import jax.numpy as jnp
from jax import lax
from jax.sharding import PartitionSpec as P

GROUP = 16
BLOCK = 128
LAGS = 8


def from_behind(value, axis, steps):
    count = lax.axis_size(axis)
    leading, last = (max(0, -steps), min(count, count - steps))
    return lax.ppermute(value, axis, [(source, source + steps) for source in range(leading, last)])


def all_toeplitz(padded, width, count):
    lag_part = jnp.arange(count, dtype=jnp.int32)[:, None, None] * width
    row_part = jnp.arange(width, dtype=jnp.int32)[None, :, None]
    col_part = jnp.arange(width, dtype=jnp.int32)[None, None, :]
    indices = lag_part + width + row_part - col_part
    return jnp.take(padded, indices, axis=1)


def per_device(query, key, value, filter_taps, skip):
    rows = query.shape[0]
    channels = query.shape[1]
    groups = channels // GROUP
    all_taps = lax.all_gather(filter_taps, "ctx", axis=0, tiled=True)
    mixed = (key.astype(jnp.float32) * value.astype(jnp.float32)).astype(jnp.bfloat16)
    mixed_cols = mixed.T.reshape(groups, GROUP, rows)
    padded = jnp.concatenate(
        [
            jnp.zeros((groups, BLOCK), jnp.bfloat16),
            all_taps.T,
            jnp.zeros((groups, BLOCK), jnp.bfloat16),
        ],
        axis=1,
    )
    toeplitz_all = all_toeplitz(padded, BLOCK, LAGS)

    def convolve(lag_index, source):
        return jnp.einsum(
            "gts,gcs->gct", toeplitz_all[:, lag_index], source, preferred_element_type=jnp.float32
        )

    summed = convolve(0, mixed_cols)
    moving = mixed_cols
    for lag_index in range(1, LAGS):
        moving = from_behind(moving, "ctx", 1)
        summed = summed + convolve(lag_index, moving)
    conv = summed.reshape(channels, rows).T
    gated = query.astype(jnp.float32) * (conv + skip[None, :] * mixed.astype(jnp.float32))
    return gated.astype(jnp.bfloat16)


def solution(mesh):
    placed = (P("ctx", "ch"), P("ctx", "ch"), P("ctx", "ch"), P("ctx", "ch"), P("ch"))
    return jax.shard_map(
        per_device, mesh=mesh, in_specs=placed, out_specs=P("ctx", "ch"), check_vma=False
    )
```

profile of v0, /device:TPU:128, one launch (start us, length us, event | category | flops | bytes accessed | tf_op | source)
XLA Modules:
  0.0 821.1 jit_solution(8726122279715097564)
XLA Ops:
  0.0 1.3 fusion.20
  1.3 0.3 copy.8
  1.6 5.1 collective-permute-start
  6.7 0.1 iota_add_fusion
  6.8 0.2 compare_select_fusion
  7.0 15.9 %collective-permute-done = bf16[128,16,128]{2,1,0:T(8,128)(2,1)S(1)} collective-permute-done((bf16[128,16,128]{2,1,0:T(8,128)(2,1)S(1)}, bf16[128,16,128]{2,1,0:T(8,128)(2,1)S(1)}, u32[]{:S(2)}, u32[]{:S(2)}) %collective-permute-start) | collective-permute-done | bytes 524320 | tf_op jit(solution)/shard_map/ppermute | solution.py:14
  22.9 1.9 collective-permute-start.1
  24.8 0.1 broadcast_clamp_fusion
  24.9 18.4 %collective-permute-done.1 = bf16[128,16,128]{2,1,0:T(8,128)(2,1)S(1)} collective-permute-done((bf16[128,16,128]{2,1,0:T(8,128)(2,1)S(1)}, bf16[128,16,128]{2,1,0:T(8,128)(2,1)S(1)}, u32[]{:S(2)}, u32[]{:S(2)}) %collective-permute-start.1) | collective-permute-done | bytes 524320 | tf_op jit(solution)/shard_map/ppermute | solution.py:14
  43.3 0.0 copy-start.2
  43.3 1.9 collective-permute-start.2
  45.2 183.3 %all_gather.3 = bf16[1024,128]{1,0:T(8,128)(2,1)S(1)} all-gather(bf16[16,128]{1,0:T(8,128)(2,1)} %param.8), channel_id=1, replica_groups=mesh['ctx'=64,'ch'=4] {'ctx'}, dimensions={0}, use_global_device_ids=true | all-gather | bytes 266240 | tf_op jit(solution)/shard_map/all_gather | solution.py:29
  228.5 453.9 %gather_fusion = bf16[131072,128]{1,0:T(8,128)(2,1)} fusion(bf16[128,1280]{0,1:T(8,128)(2,1)S(1)} %pad_maximum_fusion, s32[131072]{0:T(1024)S(1)} %broadcast_clamp_fusion), kind=kCustom, calls=%fused_computation | custom fusion | bytes 67633152 | tf_op jit(solution)/shard_map/jit(_take)/gather | solution.py:22
  682.4 0.0 copy-done.2
  682.4 46.0 %copy.9 = bf16[8,128,128,128]{2,1,3,0:T(8,128)(2,1)} copy(bf16[8,128,128,128]{3,2,1,0:T(8,128)(2,1)} %bitcast.61) | data formatting | bytes 67108864 | tf_op jit(solution)/shard_map/jit(_take)/gather | solution.py:22
  728.4 0.2 fusion.19
  728.7 0.0 copy-start.3
  728.7 0.0 collective-permute-done.2
  728.7 5.4 collective-permute-start.3
  734.1 23.2 %select_bitcast_fusion = bf16[128,8,128,128]{3,2,0,1:T(8,128)(2,1)} fusion(bf16[8,128,128,128]{2,1,3,0:T(8,128)(2,1)} %copy.9, pred[8,128,128]{2,1,0:T(8,128)(4,1)S(1)} %fusion.19), kind=kLoop, calls=%fused_computation.1 | loop fusion | flops 16777216 | bytes 67239936 | tf_op jit(solution)/shard_map/jit(_take)/select_n | solution.py:22
  757.3 0.0 copy-start
  757.3 0.0 copy-start.1
  757.3 0.0 copy-start.4
  757.3 4.5 fusion.7
  761.8 0.0 collective-permute-done.3
  761.8 1.9 collective-permute-start.4
  763.8 4.5 fusion.8
  768.2 0.0 copy-done.3
  768.3 4.5 fusion.9
  772.7 7.8 collective-permute-done.4
  780.6 1.9 collective-permute-start.5
  782.5 4.6 fusion.10
  787.1 4.7 fusion.11
  791.8 5.6 collective-permute-done.5
  797.4 1.9 collective-permute-start.6
  799.3 4.5 fusion.12
  803.7 4.5 fusion.13
  808.2 5.9 collective-permute-done.6
  814.1 4.5 fusion.14
  818.6 0.4 copy.10
  819.0 0.0 copy-done
  819.0 0.0 copy-done.1
  819.0 0.0 copy-done.4
  819.0 2.1 fusion.16
  (3 shorter events, 0.0 us)
Async XLA Ops:
  1.6 21.3 %collective-permute-start = (bf16[128,16,128]{2,1,0:T(8,128)(2,1)S(1)}, bf16[128,16,128]{2,1,0:T(8,128)(2,1)S(1)}, u32[]{:S(2)}, u32[]{:S(2)}) collective-permute-start(bf16[128,16,128]{2,1,0:T(8,128)(2,1)S(1)} %bitcast.64), channel_id=1, source_target_pairs={{0,4},{4,8},{8,12},{12,16},{16,20},{20,24},{24,28},{28,32},{32,36}... | collective-permute-start | bytes 1572872 | tf_op jit(solution)/shard_map/ppermute | solution.py:14
  22.9 20.4 %collective-permute-start.1 = (bf16[128,16,128]{2,1,0:T(8,128)(2,1)S(1)}, bf16[128,16,128]{2,1,0:T(8,128)(2,1)S(1)}, u32[]{:S(2)}, u32[]{:S(2)}) collective-permute-start(bf16[128,16,128]{2,1,0:T(8,128)(2,1)S(1)} %collective-permute-done), channel_id=1, source_target_pairs={{0,4},{4,8},{8,12},{12,16},{16,20},{20,24},{24,28},{28,32},{32,36}... | collective-permute-start | bytes 1572872 | tf_op jit(solution)/shard_map/ppermute | solution.py:14
  43.3 639.1 %copy-start.2 = (bf16[128,16,128]{2,1,0:T(8,128)(2,1)}, bf16[128,16,128]{2,1,0:T(8,128)(2,1)S(1)}, u32[]{:S(2)}) copy-start(bf16[128,16,128]{2,1,0:T(8,128)(2,1)S(1)} %collective-permute-done.1) | copy-start | bytes 1572868
  43.3 685.4 %collective-permute-start.2 = (bf16[128,16,128]{2,1,0:T(8,128)(2,1)S(1)}, bf16[128,16,128]{2,1,0:T(8,128)(2,1)}, u32[]{:S(2)}, u32[]{:S(2)}) collective-permute-start(bf16[128,16,128]{2,1,0:T(8,128)(2,1)S(1)} %collective-permute-done.1), channel_id=1, source_target_pairs={{0,4},{4,8},{8,12},{12,16},{16,20},{20,24},{24,28},{28,32},{32,36}... | collective-permute-start | bytes 1572872 | tf_op jit(solution)/shard_map/ppermute | solution.py:14
  728.7 39.6 %copy-start.3 = (bf16[128,16,128]{2,1,0:T(8,128)(2,1)S(1)}, bf16[128,16,128]{2,1,0:T(8,128)(2,1)}, u32[]{:S(2)}) copy-start(bf16[128,16,128]{2,1,0:T(8,128)(2,1)} %copy-done.2) | copy-start | bytes 1572868
  728.7 33.2 %collective-permute-start.3 = (bf16[128,16,128]{2,1,0:T(8,128)(2,1)}, bf16[128,16,128]{2,1,0:T(8,128)(2,1)}, u32[]{:S(2)}, u32[]{:S(2)}) collective-permute-start(bf16[128,16,128]{2,1,0:T(8,128)(2,1)} %collective-permute-done.2), channel_id=1, source_target_pairs={{0,4},{4,8},{8,12},{12,16},{16,20},{20,24},{24,28},{28,32},{32,36}... | collective-permute-start | bytes 1572872 | tf_op jit(solution)/shard_map/ppermute | solution.py:14
  757.3 61.7 %copy-start = (bf16[128,2048]{1,0:T(8,128)(2,1)S(1)}, bf16[128,2048]{1,0:T(8,128)(2,1)}, u32[]{:S(2)}) copy-start(bf16[128,2048]{1,0:T(8,128)(2,1)} %param.7) | copy-start | bytes 1572868
  757.3 61.7 %copy-start.1 = (bf16[128,2048]{1,0:T(8,128)(2,1)S(1)}, bf16[128,2048]{1,0:T(8,128)(2,1)}, u32[]{:S(2)}) copy-start(bf16[128,2048]{1,0:T(8,128)(2,1)} %param.6) | copy-start | bytes 1572868
  757.3 61.7 %copy-start.4 = (f32[2048]{0:T(1024)S(1)}, f32[2048]{0:T(1024)}, u32[]{:S(2)}) copy-start(f32[2048]{0:T(1024)} %param.9) | copy-start | bytes 24580
  761.8 18.7 %collective-permute-start.4 = (bf16[128,16,128]{2,1,0:T(8,128)(2,1)}, bf16[128,16,128]{2,1,0:T(8,128)(2,1)S(1)}, u32[]{:S(2)}, u32[]{:S(2)}) collective-permute-start(bf16[128,16,128]{2,1,0:T(8,128)(2,1)} %collective-permute-done.3), channel_id=1, source_target_pairs={{0,4},{4,8},{8,12},{12,16},{16,20},{20,24},{24,28},{28,32},{32,36}... | collective-permute-start | bytes 1572872 | tf_op jit(solution)/shard_map/ppermute | solution.py:14
  780.6 16.8 %collective-permute-start.5 = (bf16[128,16,128]{2,1,0:T(8,128)(2,1)S(1)}, bf16[128,16,128]{2,1,0:T(8,128)(2,1)S(1)}, u32[]{:S(2)}, u32[]{:S(2)}) collective-permute-start(bf16[128,16,128]{2,1,0:T(8,128)(2,1)S(1)} %collective-permute-done.4), channel_id=1, source_target_pairs={{0,4},{4,8},{8,12},{12,16},{16,20},{20,24},{24,28},{28,32},{32,36}... | collective-permute-start | bytes 1572872 | tf_op jit(solution)/shard_map/ppermute | solution.py:14
  797.4 16.8 %collective-permute-start.6 = (bf16[128,16,128]{2,1,0:T(8,128)(2,1)S(1)}, bf16[128,16,128]{2,1,0:T(8,128)(2,1)S(1)}, u32[]{:S(2)}, u32[]{:S(2)}) collective-permute-start(bf16[128,16,128]{2,1,0:T(8,128)(2,1)S(1)} %collective-permute-done.5), channel_id=1, source_target_pairs={{0,4},{4,8},{8,12},{12,16},{16,20},{20,24},{24,28},{28,32},{32,36}... | collective-permute-start | bytes 1572872 | tf_op jit(solution)/shard_map/ppermute | solution.py:14
where the time goes:
time: 823 us; the launch traced here: 821 us
  local copies, waits for them, and re-layouts  501 us (61%)
  blocking collectives  183 us (22%)
  waiting for transfers between devices  53.6 us (7%)
  matrix products  36.2 us (4%)
  other arithmetic  27.2 us (3%)
  starting transfers between devices  20.1 us (2%)
    gather x2, local copies, waits for them, and re-layouts, all_toeplitz(): return jnp.take(padded, indices, axis=1)  500 us
    all_gather x1, blocking collectives, per_device(): all_taps = lax.all_gather(filter_taps, 'ctx', axis=0, tiled=True)  183 us
    ppermute x7, waiting for transfers between devices, from_behind(): lax.ppermute(value, axis, [(source, source + steps) for source in range(l...  53.6 us
    dot_general x8, matrix products, convolve(): jnp.einsum('gts,gcs->gct', toeplitz_all[:, lag_index], source, preferred_...  36.2 us
    select_n x2, other arithmetic, all_toeplitz(): return jnp.take(padded, indices, axis=1)  23.4 us
    ppermute x7, starting transfers between devices, from_behind(): lax.ppermute(value, axis, [(source, source + steps) for source in range(l...  20.1 us
  transfers between devices with their start and end apart: 7, of which 5 were waited for; matrix products, arithmetic and copies ran while one was open for 68% of the time, Pallas kernels for 0%

commit v1 on v0

--- a/solution.py
+++ b/solution.py
@@ -26,7 +26,9 @@
     rows = query.shape[0]
     channels = query.shape[1]
     groups = channels // GROUP
-    all_taps = lax.all_gather(filter_taps, "ctx", axis=0, tiled=True)
+    all_taps = jnp.concatenate(
+        lax.all_to_all(jnp.stack([filter_taps] * lax.axis_size("ctx")), "ctx", 0, 0), axis=0
+    )
     mixed = (key.astype(jnp.float32) * value.astype(jnp.float32)).astype(jnp.bfloat16)
     mixed_cols = mixed.T.reshape(groups, GROUP, rows)
     padded = jnp.concatenate(

time: 823 us -> 642 us (0.78)
  blocking collectives: 183 us -> 0 us
  waiting for transfers between devices: 53.6 us -> 43.9 us
    all_gather x1 -> x0, blocking collectives: 183 us -> none  [per_device(): all_taps = lax.all_gather(filter_taps, 'ctx', axis=0, tiled=True)]
    all_to_all x0 -> x1, starting transfers between devices: none -> 10.7 us  [per_device(): lax.all_to_all(jnp.stack([filter_taps] * lax.axis_size('ctx')), 'ctx', 0, 0)]
    ppermute x7, waiting for transfers between devices: 53.6 us -> 43.9 us  [from_behind(): lax.ppermute(value, axis, [(source, source + steps) for source in range(l...]
  transfers between devices with their start and end apart: 7 -> 8, of which waited for: 5 -> 5; matrix products, arithmetic and copies ran while one was open for 68% -> 87% of each run, Pallas kernels for 0% -> 0%
where the time goes in v1:
time: 642 us; the launch traced here: 640 us
  local copies, waits for them, and re-layouts  505 us (79%)
  waiting for transfers between devices  43.9 us (7%)
  matrix products  36.3 us (6%)
  starting transfers between devices  27.5 us (4%)
  other arithmetic  27.2 us (4%)
    gather x2, local copies, waits for them, and re-layouts, all_toeplitz(): return jnp.take(padded, indices, axis=1)  503 us
    ppermute x7, waiting for transfers between devices, from_behind(): lax.ppermute(value, axis, [(source, source + steps) for source in range(l...  43.9 us
    dot_general x8, matrix products, convolve(): jnp.einsum('gts,gcs->gct', toeplitz_all[:, lag_index], source, preferred_...  36.3 us
    select_n x2, other arithmetic, all_toeplitz(): return jnp.take(padded, indices, axis=1)  23.4 us
    ppermute x7, starting transfers between devices, from_behind(): lax.ppermute(value, axis, [(source, source + steps) for source in range(l...  16.7 us
  transfers between devices with their start and end apart: 8, of which 5 were waited for; matrix products, arithmetic and copies ran while one was open for 87% of the time, Pallas kernels for 0%

profile of v1, /device:TPU:128, one launch (start us, length us, event | category | flops | bytes accessed | tf_op | source)
XLA Modules:
  0.0 640.2 jit_solution(329885496168630649)
XLA Ops:
  0.0 1.3 fusion.20
  1.3 0.3 copy.8
  1.6 5.1 collective-permute-start
  6.7 1.4 stack.2
  8.1 10.7 %all-to-all-start = ((bf16[64,16,128]{2,1,0:T(8,128)(2,1)}), bf16[64,16,128]{2,1,0:T(8,128)(2,1)S(1)}, u32[]{:S(2)}, u32[]{:S(2)}) async-start(bf16[64,16,128]{2,1,0:T(8,128)(2,1)} %stack.2), calls=%async_computation | async-start | bytes 524288 | tf_op jit(solution)/shard_map/all_to_all | solution.py:30
  18.9 4.4 collective-permute-done
  23.2 0.0 copy-start.2
  23.2 1.9 collective-permute-start.1
  25.2 0.1 iota_add_fusion
  25.2 0.2 compare_select_fusion
  25.5 17.8 %collective-permute-done.1 = bf16[128,16,128]{2,1,0:T(8,128)(2,1)S(1)} collective-permute-done((bf16[128,16,128]{2,1,0:T(8,128)(2,1)S(1)}, bf16[128,16,128]{2,1,0:T(8,128)(2,1)S(1)}, u32[]{:S(2)}, u32[]{:S(2)}) %collective-permute-start.1) | collective-permute-done | bytes 524320 | tf_op jit(solution)/shard_map/ppermute | solution.py:14
  43.3 0.0 copy-start.4
  43.3 1.9 collective-permute-start.2
  45.2 0.0 copy-done.2
  45.2 0.1 broadcast_clamp_fusion
  45.3 0.2 fusion.19
  45.5 0.0 all-to-all-done
  45.6 457.1 %gather_fusion = bf16[131072,128]{1,0:T(8,128)(2,1)} fusion(bf16[128,1280]{0,1:T(8,128)(2,1)S(1)} %pad_maximum_fusion, s32[131072]{0:T(1024)S(1)} %broadcast_clamp_fusion), kind=kCustom, calls=%fused_computation | custom fusion | bytes 67633152 | tf_op jit(solution)/shard_map/jit(_take)/gather | solution.py:22
  502.7 0.0 copy-done.4
  502.7 45.9 %copy.9 = bf16[8,128,128,128]{2,1,3,0:T(8,128)(2,1)} copy(bf16[8,128,128,128]{3,2,1,0:T(8,128)(2,1)} %bitcast.63) | data formatting | bytes 67108864 | tf_op jit(solution)/shard_map/jit(_take)/gather | solution.py:22
  548.5 0.0 copy-start.3
  548.6 0.0 collective-permute-done.2
  548.6 2.0 collective-permute-start.3
  550.6 23.2 %select_bitcast_fusion = bf16[128,8,128,128]{3,2,0,1:T(8,128)(2,1)} fusion(bf16[8,128,128,128]{2,1,3,0:T(8,128)(2,1)} %copy.9, pred[8,128,128]{2,1,0:T(8,128)(4,1)S(1)} %fusion.19), kind=kLoop, calls=%fused_computation.1 | loop fusion | flops 16777216 | bytes 67239936 | tf_op jit(solution)/shard_map/jit(_take)/select_n | solution.py:22
  573.8 0.0 copy-start
  573.8 0.0 copy-start.1
  573.8 0.0 copy-start.5
  573.8 4.5 fusion.7
  578.3 0.0 collective-permute-done.3
  578.3 1.9 collective-permute-start.4
  580.3 0.0 copy-done.3
  580.3 4.5 fusion.8
  584.8 4.7 fusion.9
  589.4 8.3 %collective-permute-done.4 = bf16[128,16,128]{2,1,0:T(8,128)(2,1)S(1)} collective-permute-done((bf16[128,16,128]{2,1,0:T(8,128)(2,1)}, bf16[128,16,128]{2,1,0:T(8,128)(2,1)S(1)}, u32[]{:S(2)}, u32[]{:S(2)}) %collective-permute-start.4) | collective-permute-done | bytes 524320 | tf_op jit(solution)/shard_map/ppermute | solution.py:14
  597.7 1.9 collective-permute-start.5
  599.6 4.6 fusion.10
  604.3 4.7 fusion.11
  608.9 7.0 %collective-permute-done.5 = bf16[128,16,128]{2,1,0:T(8,128)(2,1)S(1)} collective-permute-done((bf16[128,16,128]{2,1,0:T(8,128)(2,1)S(1)}, bf16[128,16,128]{2,1,0:T(8,128)(2,1)S(1)}, u32[]{:S(2)}, u32[]{:S(2)}) %collective-permute-start.5) | collective-permute-done | bytes 524320 | tf_op jit(solution)/shard_map/ppermute | solution.py:14
  615.9 1.9 collective-permute-start.6
  617.8 4.5 fusion.12
  622.3 4.5 fusion.13
  626.8 6.4 %collective-permute-done.6 = bf16[128,16,128]{2,1,0:T(8,128)(2,1)S(1)} collective-permute-done((bf16[128,16,128]{2,1,0:T(8,128)(2,1)S(1)}, bf16[128,16,128]{2,1,0:T(8,128)(2,1)S(1)}, u32[]{:S(2)}, u32[]{:S(2)}) %collective-permute-start.6) | collective-permute-done | bytes 524320 | tf_op jit(solution)/shard_map/ppermute | solution.py:14
  633.2 4.5 fusion.14
  637.7 0.4 copy.10
  638.0 0.0 copy-done
  638.0 0.0 copy-done.1
  638.0 0.0 copy-done.5
  638.0 2.1 fusion.16
  (3 shorter events, 0.0 us)
Async XLA Ops:
  1.6 21.6 %collective-permute-start = (bf16[128,16,128]{2,1,0:T(8,128)(2,1)S(1)}, bf16[128,16,128]{2,1,0:T(8,128)(2,1)S(1)}, u32[]{:S(2)}, u32[]{:S(2)}) collective-permute-start(bf16[128,16,128]{2,1,0:T(8,128)(2,1)S(1)} %bitcast.66), channel_id=1, source_target_pairs={{0,4},{4,8},{8,12},{12,16},{16,20},{20,24},{24,28},{28,32},{32,36}... | collective-permute-start | bytes 1572872 | tf_op jit(solution)/shard_map/ppermute | solution.py:14
  8.1 37.4 %all-to-all-start = ((bf16[64,16,128]{2,1,0:T(8,128)(2,1)}), bf16[64,16,128]{2,1,0:T(8,128)(2,1)S(1)}, u32[]{:S(2)}, u32[]{:S(2)}) async-start(bf16[64,16,128]{2,1,0:T(8,128)(2,1)} %stack.2), calls=%async_computation | async-start | bytes 524288 | tf_op jit(solution)/shard_map/all_to_all | solution.py:30
  23.2 22.0 %copy-start.2 = (bf16[128,16,128]{2,1,0:T(8,128)(2,1)}, bf16[128,16,128]{2,1,0:T(8,128)(2,1)S(1)}, u32[]{:S(2)}) copy-start(bf16[128,16,128]{2,1,0:T(8,128)(2,1)S(1)} %collective-permute-done) | copy-start | bytes 1572868
  23.2 20.0 %collective-permute-start.1 = (bf16[128,16,128]{2,1,0:T(8,128)(2,1)S(1)}, bf16[128,16,128]{2,1,0:T(8,128)(2,1)S(1)}, u32[]{:S(2)}, u32[]{:S(2)}) collective-permute-start(bf16[128,16,128]{2,1,0:T(8,128)(2,1)S(1)} %collective-permute-done), channel_id=1, source_target_pairs={{0,4},{4,8},{8,12},{12,16},{16,20},{20,24},{24,28},{28,32},{32,36}... | collective-permute-start | bytes 1572872 | tf_op jit(solution)/shard_map/ppermute | solution.py:14
  43.3 459.4 %copy-start.4 = (bf16[128,16,128]{2,1,0:T(8,128)(2,1)}, bf16[128,16,128]{2,1,0:T(8,128)(2,1)S(1)}, u32[]{:S(2)}) copy-start(bf16[128,16,128]{2,1,0:T(8,128)(2,1)S(1)} %collective-permute-done.1) | copy-start | bytes 1572868
  43.3 505.3 %collective-permute-start.2 = (bf16[128,16,128]{2,1,0:T(8,128)(2,1)S(1)}, bf16[128,16,128]{2,1,0:T(8,128)(2,1)}, u32[]{:S(2)}, u32[]{:S(2)}) collective-permute-start(bf16[128,16,128]{2,1,0:T(8,128)(2,1)S(1)} %collective-permute-done.1), channel_id=1, source_target_pairs={{0,4},{4,8},{8,12},{12,16},{16,20},{20,24},{24,28},{28,32},{32,36}... | collective-permute-start | bytes 1572872 | tf_op jit(solution)/shard_map/ppermute | solution.py:14
  548.5 31.7 %copy-start.3 = (bf16[128,16,128]{2,1,0:T(8,128)(2,1)S(1)}, bf16[128,16,128]{2,1,0:T(8,128)(2,1)}, u32[]{:S(2)}) copy-start(bf16[128,16,128]{2,1,0:T(8,128)(2,1)} %copy-done.2) | copy-start | bytes 1572868
  548.6 29.8 %collective-permute-start.3 = (bf16[128,16,128]{2,1,0:T(8,128)(2,1)}, bf16[128,16,128]{2,1,0:T(8,128)(2,1)}, u32[]{:S(2)}, u32[]{:S(2)}) collective-permute-start(bf16[128,16,128]{2,1,0:T(8,128)(2,1)} %collective-permute-done.2), channel_id=1, source_target_pairs={{0,4},{4,8},{8,12},{12,16},{16,20},{20,24},{24,28},{28,32},{32,36}... | collective-permute-start | bytes 1572872 | tf_op jit(solution)/shard_map/ppermute | solution.py:14
  573.8 64.2 %copy-start = (bf16[128,2048]{1,0:T(8,128)(2,1)S(1)}, bf16[128,2048]{1,0:T(8,128)(2,1)}, u32[]{:S(2)}) copy-start(bf16[128,2048]{1,0:T(8,128)(2,1)} %param.7) | copy-start | bytes 1572868
  573.8 64.2 %copy-start.1 = (bf16[128,2048]{1,0:T(8,128)(2,1)S(1)}, bf16[128,2048]{1,0:T(8,128)(2,1)}, u32[]{:S(2)}) copy-start(bf16[128,2048]{1,0:T(8,128)(2,1)} %param.6) | copy-start | bytes 1572868
  573.8 64.3 %copy-start.5 = (f32[2048]{0:T(1024)S(1)}, f32[2048]{0:T(1024)}, u32[]{:S(2)}) copy-start(f32[2048]{0:T(1024)} %param.9) | copy-start | bytes 24580
  578.3 19.4 %collective-permute-start.4 = (bf16[128,16,128]{2,1,0:T(8,128)(2,1)}, bf16[128,16,128]{2,1,0:T(8,128)(2,1)S(1)}, u32[]{:S(2)}, u32[]{:S(2)}) collective-permute-start(bf16[128,16,128]{2,1,0:T(8,128)(2,1)} %collective-permute-done.3), channel_id=1, source_target_pairs={{0,4},{4,8},{8,12},{12,16},{16,20},{20,24},{24,28},{28,32},{32,36}... | collective-permute-start | bytes 1572872 | tf_op jit(solution)/shard_map/ppermute | solution.py:14
  597.7 18.2 %collective-permute-start.5 = (bf16[128,16,128]{2,1,0:T(8,128)(2,1)S(1)}, bf16[128,16,128]{2,1,0:T(8,128)(2,1)S(1)}, u32[]{:S(2)}, u32[]{:S(2)}) collective-permute-start(bf16[128,16,128]{2,1,0:T(8,128)(2,1)S(1)} %collective-permute-done.4), channel_id=1, source_target_pairs={{0,4},{4,8},{8,12},{12,16},{16,20},{20,24},{24,28},{28,32},{32,36}... | collective-permute-start | bytes 1572872 | tf_op jit(solution)/shard_map/ppermute | solution.py:14
  615.9 17.3 %collective-permute-start.6 = (bf16[128,16,128]{2,1,0:T(8,128)(2,1)S(1)}, bf16[128,16,128]{2,1,0:T(8,128)(2,1)S(1)}, u32[]{:S(2)}, u32[]{:S(2)}) collective-permute-start(bf16[128,16,128]{2,1,0:T(8,128)(2,1)S(1)} %collective-permute-done.5), channel_id=1, source_target_pairs={{0,4},{4,8},{8,12},{12,16},{16,20},{20,24},{24,28},{28,32},{32,36}... | collective-permute-start | bytes 1572872 | tf_op jit(solution)/shard_map/ppermute | solution.py:14
